TPU v7x, 256 devices: a whole 4x4x8 slice. The times are simulated.
256 devices in a mesh: dom: 64 (over z, y, core), grp: 4 (over x).
Axes of the slice: x: 4, y: 4, z: 8, core: 2. Of those that a mesh axis runs over, the one named last changes fastest.
Arguments:
- features: bfloat16 [4, 65536, 512], P('grp', 'dom'), may hold values from -6 to 6
- history: bfloat16 [2, 4, 65536, 512], P(None, 'grp', 'dom'), may hold values from -6 to 6
- adj_tiles: bfloat16 [4, 512, 4, 128, 128], P('grp', 'dom'), may hold values from -0.25 to 0.25
- blocks: int32 [4, 512, 4], P('grp', 'dom'), may hold values from 0 to 11, as said below
- send_list: int32 [4, 64, 64, 8], P('grp', 'dom'), may hold values from 0 to 1023
- counts: int32 [4, 64, 64], P('grp', 'dom'), may hold values from 0 to 8, as said below
- weights: bfloat16 [3, 512, 512], replicated, may hold values from -0.25 to 0.25
- cotangent: bfloat16 [4, 65536, 512], P('grp', 'dom'), may hold values from -16 to 16
Outputs:
- embedding: bfloat16 [4, 65536, 512], P('grp', 'dom')
- fresh_halo: bfloat16 [2, 4, 32768, 512], P(None, 'grp', 'dom')
- weight_grads: float32 [3, 512, 512], P(None, 'dom')
Inputs may be any that keep to these rules, and one draw needn't show every extreme that they name: `send_list`: entries at or past counts are not read. counts[g, q, p] is zero where q equals p; some owner uses all 8 slots for every other partition, and some partition gets 8 rows from every other owner. Entry 0 of the list of a partition's block b is b itself; entries 2 and 3 name halo blocks, at least 8.
All inputs are finite; a program needn't handle non-finite values.
Results may differ from a plain program's by a relative error of at most 0.012.
Values may be sent and summed in bfloat16 or wider, within the bound.
A program may use at most 128 MiB of HBM per device.

v0:
```python
import math

import jax
import jax.numpy as jnp
from jax import lax
from jax.sharding import PartitionSpec as P


def silu_slope(values):
    sigmoid_part = jax.nn.sigmoid(values)
    return sigmoid_part * (1.0 + values * (1.0 - sigmoid_part))


def pack_rows(source_rows, send_rows, live_counts):
    peer_count = send_rows.shape[0]
    capacity = send_rows.shape[1]
    picked = jnp.take(source_rows, send_rows.reshape(-1), axis=0)
    picked = picked.reshape(peer_count, capacity, source_rows.shape[1])
    in_use = jnp.arange(capacity, dtype=jnp.int32)[None, :] < live_counts[:, None]
    return jnp.where(in_use[:, :, None], picked, jnp.zeros((), jnp.bfloat16))


def aggregate(local_rows, halo_rows, tile_set, block_set):
    block_rows = tile_set.shape[-1]
    row_width = local_rows.shape[1]
    source = jnp.concatenate([local_rows, halo_rows], axis=0).reshape(-1, block_rows, row_width)
    picked = jnp.take(source, block_set.reshape(-1), axis=0)
    picked = picked.reshape(block_set.shape + (block_rows, row_width))
    mixed = jnp.einsum("bkij,bkjd->bid", tile_set, picked, preferred_element_type=jnp.float32)
    return mixed.reshape(-1, row_width)


def spread_back(grad_rows, tile_set, block_set):
    block_rows = tile_set.shape[-1]
    row_width = grad_rows.shape[1]
    local_blocks = grad_rows.shape[0] // block_rows
    by_block = grad_rows.reshape(-1, block_rows, row_width)
    contrib_terms = jnp.einsum(
        "bkij,bid->bkjd", tile_set, by_block, preferred_element_type=jnp.float32
    )
    owners = (
        block_set.reshape(1, -1) == jnp.arange(local_blocks, dtype=jnp.int32)[:, None]
    ).astype(jnp.float32)
    summed = jnp.dot(
        owners,
        contrib_terms.reshape(owners.shape[1], -1),
        precision=lax.Precision.HIGHEST,
        preferred_element_type=jnp.float32,
    )
    return summed.reshape(-1, row_width)


def body(features, history, adj_tiles, blocks, send_list, counts, weights, cotangent):
    node_rows = features[0]
    tile_set = adj_tiles[0]
    block_set = blocks[0]
    send_rows = send_list[0, 0]
    live_counts = counts[0, 0]
    row_width = node_rows.shape[1]
    pulled = (
        lax.all_to_all(
            pack_rows(node_rows, send_rows, live_counts),
            "dom",
            split_axis=0,
            concat_axis=0,
            tiled=True,
        ),
        lax.all_to_all(
            pack_rows(history[0, 0], send_rows, live_counts),
            "dom",
            split_axis=0,
            concat_axis=0,
            tiled=True,
        ),
        lax.all_to_all(
            pack_rows(history[1, 0], send_rows, live_counts),
            "dom",
            split_axis=0,
            concat_axis=0,
            tiled=True,
        ),
    )
    halo_inputs = [piece.reshape(-1, row_width) for piece in pulled]
    current = node_rows
    aggregated = []
    linear_out = []
    hidden_rows = []
    fresh_parts = []
    for layer_index in range(3):
        mixed = aggregate(current, halo_inputs[layer_index], tile_set, block_set).astype(
            jnp.bfloat16
        )
        product = jnp.dot(mixed, weights[layer_index], preferred_element_type=jnp.float32)
        aggregated.append(mixed)
        linear_out.append(product)
        if layer_index < 2:
            current = jax.nn.silu(product).astype(jnp.bfloat16)
            hidden_rows.append(current)
    node_out = linear_out[2].astype(jnp.bfloat16)
    fresh_parts = list(
        (
            lax.all_to_all(
                pack_rows(hidden_rows[0], send_rows, live_counts),
                "dom",
                split_axis=0,
                concat_axis=0,
                tiled=True,
            ),
            lax.all_to_all(
                pack_rows(hidden_rows[1], send_rows, live_counts),
                "dom",
                split_axis=0,
                concat_axis=0,
                tiled=True,
            ),
        )
    )
    fresh_halo = jnp.stack([piece.reshape(-1, row_width) for piece in fresh_parts])
    upstream = cotangent[0]
    partial_sums = [None, None, None]
    for layer_index in (2, 1, 0):
        partial_sums[layer_index] = lax.dot_general(
            aggregated[layer_index],
            upstream,
            (((0,), (0,)), ((), ())),
            preferred_element_type=jnp.float32,
        )
        if layer_index > 0:
            slope_in = lax.dot_general(
                upstream,
                weights[layer_index],
                (((1,), (1,)), ((), ())),
                preferred_element_type=jnp.float32,
            ).astype(jnp.bfloat16)
            back_rows = spread_back(slope_in, tile_set, block_set)
            upstream = (back_rows * silu_slope(linear_out[layer_index - 1])).astype(jnp.bfloat16)
    total_rows = lax.axis_size("grp") * lax.axis_size("dom") * node_rows.shape[0]
    stacked = jnp.stack(partial_sums) * (1.0 / math.sqrt(total_rows))
    replica_total = lax.psum(stacked.astype(jnp.bfloat16), "grp").astype(jnp.float32)
    weight_grads = lax.psum_scatter(replica_total, "dom", scatter_dimension=1, tiled=True)
    return (node_out[None], fresh_halo[:, None], weight_grads)


def solution(mesh):
    placed = (
        P("grp", "dom", None),
        P(None, "grp", "dom", None),
        P("grp", "dom", None, None, None),
        P("grp", "dom", None),
        P("grp", "dom", None, None),
        P("grp", "dom", None),
        P(),
        P("grp", "dom", None),
    )
    return jax.shard_map(
        body,
        mesh=mesh,
        in_specs=placed,
        out_specs=(P("grp", "dom", None), P(None, "grp", "dom", None), P(None, "dom", None)),
        check_vma=False,
    )
```

profile of v0, /device:TPU:2, one launch (start us, length us, event | category | flops | bytes accessed | tf_op | source)
XLA Modules:
  0.0 373.9 jit_solution(13997142385125871676)
XLA Ops:
  8.9 3.3 gather_fusion
  13.3 12.4 %all-to-all-start = ((bf16[64,8,512]{2,1,0:T(8,128)(2,1)}), bf16[64,8,512]{2,1,0:T(8,128)(2,1)}, u32[]{:S(2)}, u32[]{:S(2)}) async-start(bf16[64,8,512]{2,1,0:T(8,128)(2,1)} %bitcast_select_fusion.4), calls=%async_computation | async-start | bytes 1048576 | tf_op jit(solution)/shard_map/all_to_all | solution.py:61
  32.8 10.4 %all-to-all-done = bf16[64,8,512]{2,1,0:T(8,128)(2,1)} async-done(((bf16[64,8,512]{2,1,0:T(8,128)(2,1)}), bf16[64,8,512]{2,1,0:T(8,128)(2,1)}, u32[]{:S(2)}, u32[]{:S(2)}) %all-to-all-start) | async-done | bytes 524320 | tf_op jit(solution)/shard_map/all_to_all | solution.py:61
  45.5 4.2 %gather_fusion.1 = bf16[32,128,512]{2,1,0:T(8,128)(2,1)} fusion(bf16[12,128,512]{2,1,0:T(8,128)(2,1)} %bitcast.138, s32[1024]{0:T(1024)S(1)} %pad_clamp_fusion), kind=kCustom, calls=%fused_computation.1.clone | custom fusion | bytes 8388736 | tf_op jit(solution)/shard_map/jit(_take)/gather | solution.py:27
  53.0 3.7 multiply_convert_fusion.3
  61.8 6.0 %all-to-all-start.1 = ((bf16[64,8,512]{2,1,0:T(8,128)(2,1)}), bf16[64,8,512]{2,1,0:T(8,128)(2,1)S(1)}, u32[]{:S(2)}, u32[]{:S(2)}) async-start(bf16[64,8,512]{2,1,0:T(8,128)(2,1)} %get-tuple-element.10), calls=%async_computation.1 | async-start | bytes 1048576 | tf_op jit(solution)/shard_map/all_to_all | solution.py:68
  69.9 4.5 %convolution_bitcast_fusion.1 = f32[8,4,128,512]{2,3,1,0:T(8,128)} fusion(bf16[8,128,512,1]{2,1,3,0:T(8,128)(2,1)S(1)} %bitcast.150, bf16[1,8,4,128,128]{4,3,2,1,0:T(8,128)(2,1)S(1)} %copy-done), kind=kOutput, calls=%fused_computation.12 | convolution fusion | flops 536870912 | bytes 10485760 | tf_op jit(solution)/shard_map/bkij,bid->bkjd/dot_general | solution.py:38
  74.4 10.4 %copy.29 = f32[4,8,128,512]{3,1,2,0:T(8,128)} copy(f32[4,8,128,512]{2,3,1,0:T(8,128)} %bitcast.127) | data formatting | bytes 16777216
  84.8 7.5 %fusion.22 = f32[8,65536]{1,0:T(8,128)} fusion(f32[32,65536]{1,0:T(8,128)} %bitcast.130, s32[32]{0:T(128)S(1)} %reshape_squeeze.5), kind=kOutput, calls=%fused_computation.67 | convolution fusion | flops 201326848 | bytes 10485888 | tf_op jit(solution)/shard_map/dot_general | solution.py:44
  95.6 10.1 %all-to-all-start.2 = ((bf16[64,8,512]{2,1,0:T(8,128)(2,1)}), bf16[64,8,512]{2,1,0:T(8,128)(2,1)S(1)}, u32[]{:S(2)}, u32[]{:S(2)}) async-start(bf16[64,8,512]{2,1,0:T(8,128)(2,1)} %get-tuple-element.11), calls=%async_computation.2 | async-start | bytes 1048576 | tf_op jit(solution)/shard_map/all_to_all | solution.py:75
  107.3 4.2 %gather_fusion.3 = bf16[32,128,512]{2,1,0:T(8,128)(2,1)} fusion(bf16[12,128,512]{2,1,0:T(8,128)(2,1)} %bitcast.136, s32[1024]{0:T(1024)S(1)} %pad_clamp_fusion), kind=kCustom, calls=%fused_computation.6.clone | custom fusion | bytes 8388736 | tf_op jit(solution)/shard_map/jit(_take)/gather | solution.py:27
  124.7 4.2 %gather_fusion.5 = bf16[32,128,512]{2,1,0:T(8,128)(2,1)} fusion(bf16[12,128,512]{2,1,0:T(8,128)(2,1)} %bitcast.137, s32[1024]{0:T(1024)S(1)} %pad_clamp_fusion), kind=kCustom, calls=%fused_computation.7.clone | custom fusion | bytes 8388736 | tf_op jit(solution)/shard_map/jit(_take)/gather | solution.py:27
  134.4 4.5 %convolution_bitcast_fusion = f32[8,4,128,512]{2,3,1,0:T(8,128)} fusion(bf16[8,128,512,1]{2,1,3,0:T(8,128)(2,1)S(1)} %bitcast.149, bf16[1,8,4,128,128]{4,3,2,1,0:T(8,128)(2,1)S(1)} %copy-done), kind=kOutput, calls=%fused_computation.11 | convolution fusion | flops 536870912 | bytes 10485760 | tf_op jit(solution)/shard_map/bkij,bid->bkjd/dot_general | solution.py:38
  139.0 10.4 %copy.30 = f32[4,8,128,512]{3,1,2,0:T(8,128)} copy(f32[4,8,128,512]{2,3,1,0:T(8,128)} %bitcast.128) | data formatting | bytes 16777216
  149.3 7.5 %fusion.21 = f32[8,65536]{1,0:T(8,128)} fusion(f32[32,65536]{1,0:T(8,128)} %bitcast.129, s32[32]{0:T(128)S(1)} %reshape_squeeze.5), kind=kOutput, calls=%fused_computation.66 | convolution fusion | flops 201326848 | bytes 10485888 | tf_op jit(solution)/shard_map/dot_general | solution.py:44
  156.8 3.4 reshape.129
  160.3 3.5 convolution_bitcast_fusion.4
  165.5 53.5 %all-reduce.2.cloned.1.call-done = bf16[3,512,512]{2,1,0:T(8,128)(2,1)} async-done(((bf16[3,512,512]{2,1,0:T(8,128)(2,1)}), bf16[3,512,512]{2,1,0:T(8,128)(2,1)}) %all-reduce.2.cloned.1.call-update) | async-done | bytes 1572880 | tf_op jit(solution)/shard_map/psum | solution.py:139
  219.0 3.5 convert_element_type.78
  222.5 10.7 %all-to-all-start.3 = ((bf16[64,8,512]{2,1,0:T(8,128)(2,1)}), bf16[64,8,512]{2,1,0:T(8,128)(2,1)S(1)}, u32[]{:S(2)}, u32[]{:S(2)}) async-start(bf16[64,8,512]{2,1,0:T(8,128)(2,1)} %get-tuple-element.9), calls=%async_computation.3 | async-start | bytes 1048576 | tf_op jit(solution)/shard_map/all_to_all | solution.py:102
  236.3 14.7 %all-to-all-done.3 = bf16[64,8,512]{2,1,0:T(8,128)(2,1)S(1)} async-done(((bf16[64,8,512]{2,1,0:T(8,128)(2,1)}), bf16[64,8,512]{2,1,0:T(8,128)(2,1)S(1)}, u32[]{:S(2)}, u32[]{:S(2)}) %all-to-all-start.3) | async-done | bytes 524320 | tf_op jit(solution)/shard_map/all_to_all | solution.py:102
  250.9 5.8 %all-to-all-start.4 = ((bf16[64,8,512]{2,1,0:T(8,128)(2,1)}), bf16[64,8,512]{2,1,0:T(8,128)(2,1)S(1)}, u32[]{:S(2)}, u32[]{:S(2)}) async-start(bf16[64,8,512]{2,1,0:T(8,128)(2,1)} %bitcast_select_fusion), calls=%async_computation.4 | async-start | bytes 1048576 | tf_op jit(solution)/shard_map/all_to_all | solution.py:109
  259.8 14.6 %all-to-all-done.4 = bf16[64,8,512]{2,1,0:T(8,128)(2,1)S(1)} async-done(((bf16[64,8,512]{2,1,0:T(8,128)(2,1)}), bf16[64,8,512]{2,1,0:T(8,128)(2,1)S(1)}, u32[]{:S(2)}, u32[]{:S(2)}) %all-to-all-start.4) | async-done | bytes 524320 | tf_op jit(solution)/shard_map/all_to_all | solution.py:109
  275.4 91.7 %reduce-scatter.2.cloned.1.call-done = f32[3,8,512]{2,1,0:T(8,128)} async-done(((f32[3,512,512]{2,1,0:T(8,128)}), f32[3,8,512]{2,1,0:T(8,128)}) %reduce-scatter.2.cloned.1.call-update) | async-done | bytes 49168 | tf_op jit(solution)/shard_map/reduce_scatter | solution.py:140
  (71 shorter events, 55.1 us)
Async XLA Ops:
  7.2 45.1 %copy-start = (bf16[1,8,4,128,128]{4,3,2,1,0:T(8,128)(2,1)S(1)}, bf16[1,8,4,128,128]{4,3,2,1,0:T(8,128)(2,1)}, u32[]{:S(2)}) copy-start(bf16[1,8,4,128,128]{4,3,2,1,0:T(8,128)(2,1)} %param.14) | copy-start | bytes 3145732
  12.3 13.4 %copy-start.11 = (s32[1,8,4]{1,2,0:T(4,128)S(1)}, s32[1,8,4]{1,2,0:T(4,128)}, u32[]{:S(2)}) copy-start(s32[1,8,4]{1,2,0:T(4,128)} %param.15) | copy-start | bytes 388
  13.3 29.9 %all-to-all-start = ((bf16[64,8,512]{2,1,0:T(8,128)(2,1)}), bf16[64,8,512]{2,1,0:T(8,128)(2,1)}, u32[]{:S(2)}, u32[]{:S(2)}) async-start(bf16[64,8,512]{2,1,0:T(8,128)(2,1)} %bitcast_select_fusion.4), calls=%async_computation | async-start | bytes 1048576 | tf_op jit(solution)/shard_map/all_to_all | solution.py:61
  30.1 13.0 %copy-start.1 = (bf16[1,1024,512]{2,1,0:T(8,128)(2,1)S(1)}, bf16[1,1024,512]{2,1,0:T(8,128)(2,1)}, u32[]{:S(2)}) copy-start(bf16[1,1024,512]{2,1,0:T(8,128)(2,1)} %param.12) | copy-start | bytes 3145732
  53.0 3.7 copy-start.5
  56.7 2.6 copy-start.3
  56.7 2.6 copy-start.4
  61.8 33.8 %all-to-all-start.1 = ((bf16[64,8,512]{2,1,0:T(8,128)(2,1)}), bf16[64,8,512]{2,1,0:T(8,128)(2,1)S(1)}, u32[]{:S(2)}, u32[]{:S(2)}) async-start(bf16[64,8,512]{2,1,0:T(8,128)(2,1)} %get-tuple-element.10), calls=%async_computation.1 | async-start | bytes 1048576 | tf_op jit(solution)/shard_map/all_to_all | solution.py:68
  95.6 27.8 %all-to-all-start.2 = ((bf16[64,8,512]{2,1,0:T(8,128)(2,1)}), bf16[64,8,512]{2,1,0:T(8,128)(2,1)S(1)}, u32[]{:S(2)}, u32[]{:S(2)}) async-start(bf16[64,8,512]{2,1,0:T(8,128)(2,1)} %get-tuple-element.11), calls=%async_computation.2 | async-start | bytes 1048576 | tf_op jit(solution)/shard_map/all_to_all | solution.py:75
  105.7 113.3 %all-reduce.2.cloned.1.call-start = ((), (), s32[]{:S(2)}) async-start(), calls=%async_computation.6 | async-start | bytes 3145728 | tf_op jit(solution)/shard_map/psum | solution.py:139
  114.1 1.6 copy-start.2
  114.1 2.0 copy-start.12
  131.5 1.2 copy-start.13
  132.2 2.2 copy-start.7
  132.7 1.7 copy-start.8
  156.8 3.4 copy-start.6
  160.3 3.5 copy-start.9
  160.3 3.5 copy-start.10
  165.4 201.7 %reduce-scatter.2.cloned.1.call-start = ((), (), s32[]{:S(2)}) async-start(), calls=%async_computation.7 | async-start | bytes 3194880 | tf_op jit(solution)/shard_map/reduce_scatter | solution.py:140
  222.5 28.4 %all-to-all-start.3 = ((bf16[64,8,512]{2,1,0:T(8,128)(2,1)}), bf16[64,8,512]{2,1,0:T(8,128)(2,1)S(1)}, u32[]{:S(2)}, u32[]{:S(2)}) async-start(bf16[64,8,512]{2,1,0:T(8,128)(2,1)} %get-tuple-element.9), calls=%async_computation.3 | async-start | bytes 1048576 | tf_op jit(solution)/shard_map/all_to_all | solution.py:102
  250.9 23.4 %all-to-all-start.4 = ((bf16[64,8,512]{2,1,0:T(8,128)(2,1)}), bf16[64,8,512]{2,1,0:T(8,128)(2,1)S(1)}, u32[]{:S(2)}, u32[]{:S(2)}) async-start(bf16[64,8,512]{2,1,0:T(8,128)(2,1)} %bitcast_select_fusion), calls=%async_computation.4 | async-start | bytes 1048576 | tf_op jit(solution)/shard_map/all_to_all | solution.py:109
Sparse Core Ops, SparseCore 0:
  165.5 53.4 all-reduce.1
  223.7 143.3 reduce-scatter.1
where the time goes:
time: 375 us; the launch traced here: 374 us
  waiting for transfers between devices  187 us (50%)
  local copies, waits for them, and re-layouts  57.8 us (15%)
  starting transfers between devices  45.3 us (12%)
  matrix products  45.1 us (12%)
  other arithmetic  24.2 us (6%)
  between operations  14.3 us (4%)
    reduce_scatter x1, waiting for transfers between devices, body(): lax.psum_scatter(replica_total, 'dom', scatter_dimension=1, tiled=True)  91.7 us
    psum x1, waiting for transfers between devices, body(): lax.psum(stacked.astype(jnp.bfloat16), 'grp').astype(jnp.float32)  53.5 us
    unnamed x32, local copies, waits for them, and re-layouts  23.5 us
    dot_general x2, matrix products, spread_back(): jnp.dot(owners, contrib_terms.reshape(owners.shape[1], -1), precision=lax...  15 us
    all_to_all x1, waiting for transfers between devices, body(): lax.all_to_all(pack_rows(hidden_rows[0], send_rows, live_counts), 'dom',...  14.7 us
    all_to_all x1, waiting for transfers between devices, body(): lax.all_to_all(pack_rows(hidden_rows[1], send_rows, live_counts), 'dom',...  14.6 us
    gather x5, local copies, waits for them, and re-layouts, pack_rows(): picked = jnp.take(source_rows, send_rows.reshape(-1), axis=0)  13.2 us
    gather x3, local copies, waits for them, and re-layouts, aggregate(): picked = jnp.take(source, block_set.reshape(-1), axis=0)  12.5 us
  transfers between devices with their start and end apart: 7, of which 6 were waited for; matrix products, arithmetic and copies ran while one was open for 15% of the time, Pallas kernels for 0%

commit v1 on v0

--- a/solution.py
+++ b/solution.py
@@ -136,8 +136,11 @@
             upstream = (back_rows * silu_slope(linear_out[layer_index - 1])).astype(jnp.bfloat16)
     total_rows = lax.axis_size("grp") * lax.axis_size("dom") * node_rows.shape[0]
     stacked = jnp.stack(partial_sums) * (1.0 / math.sqrt(total_rows))
-    replica_total = lax.psum(stacked.astype(jnp.bfloat16), "grp").astype(jnp.float32)
-    weight_grads = lax.psum_scatter(replica_total, "dom", scatter_dimension=1, tiled=True)
+    n_dom = lax.axis_size("dom")
+    pieces = stacked.astype(jnp.bfloat16).reshape(3, n_dom, -1, row_width).transpose(1, 0, 2, 3)
+    arrived = lax.all_to_all(pieces, "dom", split_axis=0, concat_axis=0, tiled=True)
+    dom_total = jnp.sum(arrived.astype(jnp.float32), axis=0)
+    weight_grads = lax.psum(dom_total, "grp")
     return (node_out[None], fresh_halo[:, None], weight_grads)
 
 

time: 375 us -> 261 us (0.70)
  waiting for transfers between devices: 187 us -> 48.4 us
  blocking collectives: 0 us -> 15 us
  between operations: 14.3 us -> 0.87 us
  starting transfers between devices: 45.3 us -> 56.9 us
  matrix products: 45.1 us -> 49.6 us
    reduce_scatter x1 -> x0, waiting for transfers between devices: 91.7 us -> none  [body(): lax.psum_scatter(replica_total, 'dom', scatter_dimension=1, tiled=True)]
    psum x1 -> x0, waiting for transfers between devices: 53.5 us -> none  [body(): lax.psum(stacked.astype(jnp.bfloat16), 'grp').astype(jnp.float32)]
    all_to_all x0 -> x1, waiting for transfers between devices: none -> 34.8 us  [body(): lax.all_to_all(pieces, 'dom', split_axis=0, concat_axis=0, tiled=True)]
    psum x0 -> x1, blocking collectives: none -> 15 us  [body(): weight_grads = lax.psum(dom_total, 'grp')]
    all_to_all x1, waiting for transfers between devices: 14.7 us -> 0.01 us  [body(): lax.all_to_all(pack_rows(hidden_rows[0], send_rows, live_counts), 'dom',...]
    all_to_all x1, waiting for transfers between devices: 14.6 us -> 3.26 us  [body(): lax.all_to_all(pack_rows(hidden_rows[1], send_rows, live_counts), 'dom',...]
    all_to_all x0 -> x1, starting transfers between devices: none -> 6.96 us  [body(): lax.all_to_all(pieces, 'dom', split_axis=0, concat_axis=0, tiled=True)]
    convert_element_type x2 -> x0, other arithmetic: 5.11 us -> none  [the longest x1 3.49 us: body(): lax.psum(stacked.astype(jnp.bfloat16), 'grp').astype(jnp.float32)]
  transfers between devices with their start and end apart: 7 -> 6, of which waited for: 6 -> 3; matrix products, arithmetic and copies ran while one was open for 15% -> 43% of each run, Pallas kernels for 0% -> 0%
where the time goes in v1:
time: 261 us; the launch traced here: 257 us
  local copies, waits for them, and re-layouts  60.5 us (23%)
  starting transfers between devices  56.9 us (22%)
  matrix products  49.6 us (19%)
  waiting for transfers between devices  48.4 us (19%)
  other arithmetic  25.5 us (10%)
  blocking collectives  15 us (6%)
    all_to_all x1, waiting for transfers between devices, body(): lax.all_to_all(pieces, 'dom', split_axis=0, concat_axis=0, tiled=True)  34.8 us
    unnamed x20, local copies, waits for them, and re-layouts  21.8 us
    psum x1, blocking collectives, body(): weight_grads = lax.psum(dom_total, 'grp')  15 us
    gather x5, local copies, waits for them, and re-layouts, pack_rows(): picked = jnp.take(source_rows, send_rows.reshape(-1), axis=0)  13.2 us
    gather x3, local copies, waits for them, and re-layouts, aggregate(): picked = jnp.take(source, block_set.reshape(-1), axis=0)  12.5 us
    all_to_all x1, starting transfers between devices, body(): lax.all_to_all(pack_rows(node_rows, send_rows, live_counts), 'dom', split...  12.4 us
    all_to_all x1, starting transfers between devices, body(): lax.all_to_all(pack_rows(hidden_rows[0], send_rows, live_counts), 'dom',...  10.7 us
    dot_general x3, matrix products, body(): jnp.dot(mixed, weights[layer_index], preferred_element_type=jnp.float32)  10.5 us
  transfers between devices with their start and end apart: 6, of which 3 were waited for; matrix products, arithmetic and copies ran while one was open for 43% of the time, Pallas kernels for 0%

profile of v1, /device:TPU:2, one launch (start us, length us, event | category | flops | bytes accessed | tf_op | source)
XLA Modules:
  0.0 256.8 jit_solution(11787648781789888998)
XLA Ops:
  2.4 3.3 %gather_fusion = bf16[512,512]{1,0:T(8,128)(2,1)S(1)} fusion(bf16[1024,512]{1,0:T(8,128)(2,1)} %bitcast.151, s32[1024]{0:T(1024)S(1)} %pad_clamp_fusion.1), kind=kCustom, calls=%fused_computation.clone | custom fusion | bytes 1050624 | tf_op jit(solution)/shard_map/jit(_take)/gather | solution.py:17
  6.7 12.4 %all-to-all-start = ((bf16[64,8,512]{2,1,0:T(8,128)(2,1)}), bf16[64,8,512]{2,1,0:T(8,128)(2,1)}, u32[]{:S(2)}, u32[]{:S(2)}) async-start(bf16[64,8,512]{2,1,0:T(8,128)(2,1)} %bitcast_select_fusion.4), calls=%async_computation | async-start | bytes 1048576 | tf_op jit(solution)/shard_map/all_to_all | solution.py:61
  26.3 10.4 %all-to-all-done = bf16[64,8,512]{2,1,0:T(8,128)(2,1)} async-done(((bf16[64,8,512]{2,1,0:T(8,128)(2,1)}), bf16[64,8,512]{2,1,0:T(8,128)(2,1)}, u32[]{:S(2)}, u32[]{:S(2)}) %all-to-all-start) | async-done | bytes 524320 | tf_op jit(solution)/shard_map/all_to_all | solution.py:61
  38.9 4.2 %gather_fusion.1 = bf16[32,128,512]{2,1,0:T(8,128)(2,1)} fusion(bf16[12,128,512]{2,1,0:T(8,128)(2,1)} %bitcast.158, s32[1024]{0:T(1024)S(1)} %pad_clamp_fusion), kind=kCustom, calls=%fused_computation.1.clone | custom fusion | bytes 8388736 | tf_op jit(solution)/shard_map/jit(_take)/gather | solution.py:27
  46.5 3.3 %multiply_convert_fusion.3 = (bf16[1024,512]{1,0:T(8,128)(2,1)S(1)}, f32[1024,512]{1,0:T(8,128)}) fusion(bf16[1024,512]{1,0:T(8,128)(2,1)S(1)} %bitcast.161, bf16[3,512,512]{2,1,0:T(8,128)(2,1)} %param.18), kind=kOutput, calls=%fused_computation.23 | convolution fusion | flops 539492352 | bytes 4718592 | tf_op jit(solution)/shard_map/dot_general | solution.py:93
  55.2 6.2 %all-to-all-start.1 = ((bf16[64,8,512]{2,1,0:T(8,128)(2,1)}), bf16[64,8,512]{2,1,0:T(8,128)(2,1)}, u32[]{:S(2)}, u32[]{:S(2)}) async-start(bf16[64,8,512]{2,1,0:T(8,128)(2,1)} %get-tuple-element.10), calls=%async_computation.1 | async-start | bytes 1048576 | tf_op jit(solution)/shard_map/all_to_all | solution.py:68
  63.6 4.5 %convolution_bitcast_fusion.1 = f32[8,4,128,512]{2,3,1,0:T(8,128)} fusion(bf16[8,128,512,1]{2,1,3,0:T(8,128)(2,1)S(1)} %bitcast.166, bf16[1,8,4,128,128]{4,3,2,1,0:T(8,128)(2,1)S(1)} %copy-done), kind=kOutput, calls=%fused_computation.12 | convolution fusion | flops 536870912 | bytes 10485760 | tf_op jit(solution)/shard_map/bkij,bid->bkjd/dot_general | solution.py:38
  68.1 10.4 %copy.45 = f32[4,8,128,512]{3,1,2,0:T(8,128)} copy(f32[4,8,128,512]{2,3,1,0:T(8,128)} %bitcast.147) | data formatting | bytes 16777216
  78.5 7.5 %fusion.28 = f32[8,65536]{1,0:T(8,128)} fusion(f32[32,65536]{1,0:T(8,128)} %bitcast.150, s32[32]{0:T(128)S(1)} %reshape_squeeze.5), kind=kOutput, calls=%fused_computation.74 | convolution fusion | flops 201326848 | bytes 10485888 | tf_op jit(solution)/shard_map/dot_general | solution.py:44
  86.0 3.3 %reshape.152 = f32[1024,512]{1,0:T(8,128)} reshape(f32[8,65536]{1,0:T(8,128)} %fusion.28) | data formatting | bytes 4194304 | tf_op jit(solution)/shard_map/reshape | solution.py:50
  90.6 10.3 %all-to-all-start.2 = ((bf16[64,8,512]{2,1,0:T(8,128)(2,1)}), bf16[64,8,512]{2,1,0:T(8,128)(2,1)}, u32[]{:S(2)}, u32[]{:S(2)}) async-start(bf16[64,8,512]{2,1,0:T(8,128)(2,1)} %get-tuple-element.11), calls=%async_computation.2 | async-start | bytes 1048576 | tf_op jit(solution)/shard_map/all_to_all | solution.py:75
  103.2 4.2 %gather_fusion.3 = bf16[32,128,512]{2,1,0:T(8,128)(2,1)} fusion(bf16[12,128,512]{2,1,0:T(8,128)(2,1)} %bitcast.157, s32[1024]{0:T(1024)S(1)} %pad_clamp_fusion), kind=kCustom, calls=%fused_computation.6.clone | custom fusion | bytes 8388736 | tf_op jit(solution)/shard_map/jit(_take)/gather | solution.py:27
  112.1 4.1 %multiply_convert_fusion.1 = (bf16[1024,512]{1,0:T(8,128)(2,1)}, bf16[1024,512]{1,0:T(8,128)(2,1)S(1)}) fusion(f32[1024,512]{1,0:T(8,128)} %reshape.152, bf16[1024,512]{1,0:T(8,128)(2,1)S(1)} %bitcast.164, bf16[3,512,512]{2,1,0:T(8,128)(2,1)} %param.18), kind=kOutput, calls=%fused_computation.20 | convolution fusion | flops 542638080 | bytes 5767168 | tf_op jit(solution)/shard_map/dot_general | solution.py:93
  121.3 10.7 %all-to-all-start.3 = ((bf16[64,8,512]{2,1,0:T(8,128)(2,1)}), bf16[64,8,512]{2,1,0:T(8,128)(2,1)}, u32[]{:S(2)}, u32[]{:S(2)}) async-start(bf16[64,8,512]{2,1,0:T(8,128)(2,1)} %get-tuple-element.9), calls=%async_computation.3 | async-start | bytes 1048576 | tf_op jit(solution)/shard_map/all_to_all | solution.py:102
  134.4 4.2 %gather_fusion.5 = bf16[32,128,512]{2,1,0:T(8,128)(2,1)} fusion(bf16[12,128,512]{2,1,0:T(8,128)(2,1)} %bitcast.156, s32[1024]{0:T(1024)S(1)} %pad_clamp_fusion), kind=kCustom, calls=%fused_computation.7.clone | custom fusion | bytes 8388736 | tf_op jit(solution)/shard_map/jit(_take)/gather | solution.py:27
  138.5 4.7 %broadcast_select_fusion.2 = bf16[32,128,512]{2,1,0:T(8,128)(2,1)} fusion(bf16[32,128,512]{2,1,0:T(8,128)(2,1)} %gather_fusion.5, pred[32]{0:T(512)(128)(4,1)S(1)} %compare_and_fusion), kind=kLoop, calls=%fused_computation.10 | loop fusion | flops 2097152 | bytes 8388640 | tf_op jit(solution)/shard_map/jit(_take)/select_n | solution.py:27
  143.2 4.5 %convolution_bitcast_fusion = f32[8,4,128,512]{2,3,1,0:T(8,128)} fusion(bf16[8,128,512,1]{2,1,3,0:T(8,128)(2,1)S(1)} %bitcast.165, bf16[1,8,4,128,128]{4,3,2,1,0:T(8,128)(2,1)S(1)} %copy-done), kind=kOutput, calls=%fused_computation.11 | convolution fusion | flops 536870912 | bytes 10485760 | tf_op jit(solution)/shard_map/bkij,bid->bkjd/dot_general | solution.py:38
  147.8 10.4 %copy.46 = f32[4,8,128,512]{3,1,2,0:T(8,128)} copy(f32[4,8,128,512]{2,3,1,0:T(8,128)} %bitcast.148) | data formatting | bytes 16777216
  159.1 4.6 %bitcast_convert_fusion = bf16[8,512,128]{1,2,0:T(8,128)(2,1)} fusion(bf16[8,4,128,512]{3,2,1,0:T(8,128)(2,1)} %bitcast.153, bf16[1,8,4,128,128]{4,3,2,1,0:T(8,128)(2,1)S(1)} %copy-done), kind=kOutput, calls=%fused_computation.16 | convolution fusion | flops 537395200 | bytes 6291456 | tf_op jit(solution)/shard_map/bkij,bkjd->bid/dot_general | solution.py:29
  166.7 10.3 %all-to-all-start.4 = ((bf16[64,8,512]{2,1,0:T(8,128)(2,1)}), bf16[64,8,512]{2,1,0:T(8,128)(2,1)}, u32[]{:S(2)}, u32[]{:S(2)}) async-start(bf16[64,8,512]{2,1,0:T(8,128)(2,1)} %bitcast_select_fusion), calls=%async_computation.4 | async-start | bytes 1048576 | tf_op jit(solution)/shard_map/all_to_all | solution.py:109
  191.2 3.3 %all-to-all-done.4 = bf16[64,8,512]{2,1,0:T(8,128)(2,1)} async-done(((bf16[64,8,512]{2,1,0:T(8,128)(2,1)}), bf16[64,8,512]{2,1,0:T(8,128)(2,1)}, u32[]{:S(2)}, u32[]{:S(2)}) %all-to-all-start.4) | async-done | bytes 524320 | tf_op jit(solution)/shard_map/all_to_all | solution.py:109
  194.5 7.0 %all-to-all-start.5 = ((bf16[64,3,8,512]{3,2,1,0:T(8,128)(2,1)}), bf16[64,3,8,512]{3,2,1,0:T(8,128)(2,1)S(1)}, u32[]{:S(2)}, u32[]{:S(2)}) async-start(bf16[64,3,8,512]{3,2,1,0:T(8,128)(2,1)} %copy.35), calls=%async_computation.5 | async-start | bytes 3145728 | tf_op jit(solution)/shard_map/all_to_all | solution.py:141
  206.7 34.8 %all-to-all-done.5 = bf16[64,3,8,512]{3,2,1,0:T(8,128)(2,1)S(1)} async-done(((bf16[64,3,8,512]{3,2,1,0:T(8,128)(2,1)}), bf16[64,3,8,512]{3,2,1,0:T(8,128)(2,1)S(1)}, u32[]{:S(2)}, u32[]{:S(2)}) %all-to-all-start.5) | async-done | bytes 1572896 | tf_op jit(solution)/shard_map/all_to_all | solution.py:141
  241.8 15.0 %psum.7 = f32[3,8,512]{2,1,0:T(8,128)} all-reduce(f32[3,8,512]{2,1,0:T(8,128)S(1)} %convert_reduce_fusion), channel_id=1, replica_groups=mesh['dom'=64,'grp'=4] {'grp'}, use_global_device_ids=true, to_apply=%region_1.4 | all-reduce | flops 12288 | bytes 98304 | tf_op jit(solution)/shard_map/psum | solution.py:143
  (60 shorter events, 62.4 us)
Async XLA Ops:
  0.6 45.2 %copy-start = (bf16[1,8,4,128,128]{4,3,2,1,0:T(8,128)(2,1)S(1)}, bf16[1,8,4,128,128]{4,3,2,1,0:T(8,128)(2,1)}, u32[]{:S(2)}) copy-start(bf16[1,8,4,128,128]{4,3,2,1,0:T(8,128)(2,1)} %param.14) | copy-start | bytes 3145732
  5.7 13.4 %copy-start.7 = (s32[1,8,4]{1,2,0:T(4,128)S(1)}, s32[1,8,4]{1,2,0:T(4,128)}, u32[]{:S(2)}) copy-start(s32[1,8,4]{1,2,0:T(4,128)} %param.15) | copy-start | bytes 388
  6.7 29.9 %all-to-all-start = ((bf16[64,8,512]{2,1,0:T(8,128)(2,1)}), bf16[64,8,512]{2,1,0:T(8,128)(2,1)}, u32[]{:S(2)}, u32[]{:S(2)}) async-start(bf16[64,8,512]{2,1,0:T(8,128)(2,1)} %bitcast_select_fusion.4), calls=%async_computation | async-start | bytes 1048576 | tf_op jit(solution)/shard_map/all_to_all | solution.py:61
  23.6 13.0 %copy-start.2 = (bf16[1,1024,512]{2,1,0:T(8,128)(2,1)S(1)}, bf16[1,1024,512]{2,1,0:T(8,128)(2,1)}, u32[]{:S(2)}) copy-start(bf16[1,1024,512]{2,1,0:T(8,128)(2,1)} %param.12) | copy-start | bytes 3145732
  55.2 35.4 %all-to-all-start.1 = ((bf16[64,8,512]{2,1,0:T(8,128)(2,1)}), bf16[64,8,512]{2,1,0:T(8,128)(2,1)}, u32[]{:S(2)}, u32[]{:S(2)}) async-start(bf16[64,8,512]{2,1,0:T(8,128)(2,1)} %get-tuple-element.10), calls=%async_computation.1 | async-start | bytes 1048576 | tf_op jit(solution)/shard_map/all_to_all | solution.py:68
  90.6 30.7 %all-to-all-start.2 = ((bf16[64,8,512]{2,1,0:T(8,128)(2,1)}), bf16[64,8,512]{2,1,0:T(8,128)(2,1)}, u32[]{:S(2)}, u32[]{:S(2)}) async-start(bf16[64,8,512]{2,1,0:T(8,128)(2,1)} %get-tuple-element.11), calls=%async_computation.2 | async-start | bytes 1048576 | tf_op jit(solution)/shard_map/all_to_all | solution.py:75
  121.3 45.3 %all-to-all-start.3 = ((bf16[64,8,512]{2,1,0:T(8,128)(2,1)}), bf16[64,8,512]{2,1,0:T(8,128)(2,1)}, u32[]{:S(2)}, u32[]{:S(2)}) async-start(bf16[64,8,512]{2,1,0:T(8,128)(2,1)} %get-tuple-element.9), calls=%async_computation.3 | async-start | bytes 1048576 | tf_op jit(solution)/shard_map/all_to_all | solution.py:102
  138.5 4.7 %copy-start.4 = (bf16[1024,512]{1,0:T(8,128)(2,1)S(1)}, bf16[1024,512]{1,0:T(8,128)(2,1)}, u32[]{:S(2)}) copy-start(bf16[1024,512]{1,0:T(8,128)(2,1)} %convolution_convert_fusion) | copy-start | bytes 3145732
  158.1 5.6 %copy-start.1 = (f32[4,8,128,512]{3,1,2,0:T(8,128)S(1)}, f32[4,8,128,512]{3,1,2,0:T(8,128)}, u32[]{:S(2)}) copy-start(f32[4,8,128,512]{3,1,2,0:T(8,128)} %copy.46) | copy-start | bytes 25165828
  166.7 27.8 %all-to-all-start.4 = ((bf16[64,8,512]{2,1,0:T(8,128)(2,1)}), bf16[64,8,512]{2,1,0:T(8,128)(2,1)}, u32[]{:S(2)}, u32[]{:S(2)}) async-start(bf16[64,8,512]{2,1,0:T(8,128)(2,1)} %bitcast_select_fusion), calls=%async_computation.4 | async-start | bytes 1048576 | tf_op jit(solution)/shard_map/all_to_all | solution.py:109
  184.2 2.4 copy-start.3
  184.2 2.5 copy-start.5
  186.6 2.8 %copy-start.6 = (f32[1,64,8,512]{3,2,1,0:T(8,128)S(1)}, f32[1,64,8,512]{3,2,1,0:T(8,128)}, u32[]{:S(2)}) copy-start(f32[1,64,8,512]{3,2,1,0:T(8,128)} %convolution_bitcast_fusion.3) | copy-start | bytes 3145732
  194.5 47.1 %all-to-all-start.5 = ((bf16[64,3,8,512]{3,2,1,0:T(8,128)(2,1)}), bf16[64,3,8,512]{3,2,1,0:T(8,128)(2,1)S(1)}, u32[]{:S(2)}, u32[]{:S(2)}) async-start(bf16[64,3,8,512]{3,2,1,0:T(8,128)(2,1)} %copy.35), calls=%async_computation.5 | async-start | bytes 3145728 | tf_op jit(solution)/shard_map/all_to_all | solution.py:141

commit v2 on v0

v2 whole, which is shorter than its diff:
```python
import functools
import math

import jax
import jax.numpy as jnp
from jax import lax
from jax.experimental import pallas as pl
from jax.experimental.pallas import tpu as pltpu
from jax.sharding import PartitionSpec as P

MESH = pl.DeviceIdType.MESH
BF = jnp.bfloat16
F32 = jnp.float32
N_DOM, N_GRP, N_Z, N_Y = 64, 4, 8, 4
ROWS, D, HALO, CAP = 1024, 512, 512, 8
STEP = 256


def dot(a, b):
    return jnp.dot(a, b, preferred_element_type=F32)


def dot_rows(a, b):
    return lax.dot_general(a, b, (((0,), (0,)), ((), ())), preferred_element_type=F32)


def dot_t(a, b):
    return lax.dot_general(a, b, (((1,), (1,)), ((), ())), preferred_element_type=F32)


def step_kernel(
    blk, idx_h, feat_h, hist_h, adj_h, w_h, cot_h,
    emb_o, fresh_o, wg_o,
    idx, feat, hist, adj, w, cot, hot, mix, back_mix, halo, h1, h2, mid, slope0, slope1,
    dm, grad, acc, emb, send, recv,
    wg, core_in, x_out, x_in, y_out, y_in, z_out, z_in, quarters,
    in_sem, send_sem, recv_sem, core_sem, x_sem, y_sem, z_sem, q_sem, out_sem,
):
    me = lax.axis_index("dom")
    g = lax.axis_index("grp")
    z, y, c = me // 8, (me % 8) // 2, me % 2
    loads = [
        pltpu.make_async_copy(a, b, in_sem.at[i])
        for i, (a, b) in enumerate(
            [(idx_h, idx), (feat_h, feat), (hist_h.at[0], hist.at[0]), (hist_h.at[1], hist.at[1]),
             (adj_h, adj), (w_h, w), (cot_h, cot)]
        )
    ]
    for load in loads:
        load.start()

    barrier = pltpu.get_barrier_semaphore()

    def greet(s, _):
        pl.semaphore_signal(barrier, inc=1, device_id={"dom": lax.rem(me + s, N_DOM)}, device_id_type=MESH)
        return 0

    lax.fori_loop(1, N_DOM, greet, 0)
    for s in range(1, N_GRP):
        pl.semaphore_signal(barrier, inc=1, device_id={"grp": lax.rem(g + s, N_GRP)}, device_id_type=MESH)

    def gather(rows_ref, turn):
        def one(i, _):
            rows = pl.ds(pl.multiple_of(i * STEP, STEP), STEP)
            picked = dot(hot[rows, :], rows_ref[...])
            send[turn, pl.ds(i * (STEP // CAP), STEP // CAP)] = picked.reshape(STEP // CAP, CAP, D).astype(BF)
            return 0

        lax.fori_loop(0, HALO // STEP, one, 0)

    def exchange(turn):
        def one(s, _):
            half = (s + 1) // 2
            to = jnp.where(lax.rem(s, 2) == 1, lax.rem(me + half, N_DOM), lax.rem(me + N_DOM - half, N_DOM))
            pltpu.make_async_remote_copy(
                send.at[turn, to], recv.at[turn, me], send_sem.at[turn], recv_sem.at[turn],
                device_id={"dom": to}, device_id_type=MESH,
            ).start()
            return 0

        lax.fori_loop(1, N_DOM, one, 0)

    def arrived(turn):
        block = recv.at[turn, pl.ds(0, N_DOM - 1)]
        pltpu.make_async_copy(block, block, recv_sem.at[turn]).wait()

    def unpack(turn):
        def one(i, _):
            part = recv[turn, pl.ds(i * 8, 8)].astype(F32).reshape(64, D)
            halo[pl.ds(pl.multiple_of(i * 64, 64), 64), :] = part.astype(BF)
            return 0

        lax.fori_loop(0, N_DOM // 8, one, 0)

    def forward(layer, rows_ref, next_ref, slope_ref):
        def one(i, _):
            rows = pl.ds(pl.multiple_of(i * STEP, STEP), STEP)
            mixed = dot(mix[rows, 0:ROWS], rows_ref[...]) + dot(mix[rows, ROWS:ROWS + HALO], halo[...])
            mixed = mixed.astype(BF)
            mid[layer, rows, :] = mixed
            value = dot(mixed, w[layer])
            if slope_ref is None:
                next_ref[rows, :] = value.astype(BF)
            else:
                part = jax.nn.sigmoid(value)
                next_ref[rows, :] = (value * part).astype(BF)
                slope_ref[rows, :] = part * (1.0 + value * (1.0 - part))
            return 0

        lax.fori_loop(0, ROWS // STEP, one, 0)

    def back_through(layer, grad_ref):
        def one(i, _):
            rows = pl.ds(pl.multiple_of(i * STEP, STEP), STEP)
            dm[rows, :] = dot_t(grad_ref[rows, :], w[layer]).astype(BF)
            return 0

        lax.fori_loop(0, ROWS // STEP, one, 0)

    def spread(slope_ref):
        def one(i, _):
            rows = pl.ds(pl.multiple_of(i * STEP, STEP), STEP)
            grad[rows, :] = (dot(back_mix[rows, :], dm[...]) * slope_ref[rows, :]).astype(BF)
            return 0

        lax.fori_loop(0, ROWS // STEP, one, 0)

    def weight_grad(layer, grad_ref):
        acc[...] = jnp.zeros_like(acc)

        def one(i, _):
            rows = pl.ds(pl.multiple_of(i * STEP, STEP), STEP)
            acc[...] += dot_rows(mid[layer, rows, :], grad_ref[rows, :])
            return 0

        lax.fori_loop(0, ROWS // STEP, one, 0)
        wg[layer] = acc[...].reshape(32, 2, 8, D).astype(BF)
        core_copy(layer).start()

    def core_copy(layer):
        return pltpu.make_async_remote_copy(
            wg.at[layer, :, 1 - c], core_in.at[layer], core_sem.at[0, layer], core_sem.at[1, layer],
            device_id={"dom": me + 1 - 2 * c}, device_id_type=MESH,
        )

    def x_copy(layer, s):
        to = lax.rem(g + s, N_GRP)
        return pltpu.make_async_remote_copy(
            x_out.at[to, layer], x_in.at[s - 1, layer], x_sem.at[0, layer, s - 1], x_sem.at[1, layer, s - 1],
            device_id={"grp": to}, device_id_type=MESH,
        )

    def x_stage(layer):
        core_copy(layer).wait_recv()
        both = wg[layer, :, c].astype(F32) + core_in[layer].astype(F32)
        for q in range(N_GRP):
            x_out[q, layer] = both[:, :, q * 128:(q + 1) * 128].astype(BF)
        for s in range(1, N_GRP):
            x_copy(layer, s).start()

    def y_copy(s):
        to = lax.rem(y + s, N_Y)
        return pltpu.make_async_remote_copy(
            y_out.at[to], y_in.at[s - 1], y_sem.at[0, s - 1], y_sem.at[1, s - 1],
            device_id={"dom": z * 8 + to * 2 + c}, device_id_type=MESH,
        )

    def z_copy(s):
        to = lax.rem(z + s, N_Z)
        return pltpu.make_async_remote_copy(
            z_out.at[to], z_in.at[s - 1], z_sem.at[0, s - 1], z_sem.at[1, s - 1],
            device_id={"dom": to * 8 + y * 2 + c}, device_id_type=MESH,
        )

    def q_copy(s):
        return pltpu.make_async_remote_copy(
            quarters.at[g], quarters.at[g], q_sem.at[0, s - 1], q_sem.at[1, s - 1],
            device_id={"grp": lax.rem(g + s, N_GRP)}, device_id_type=MESH,
        )

    def y_prepare(layer):
        for s in range(1, N_GRP):
            x_copy(layer, s).wait_recv()
        total = x_out[g, layer].astype(F32)
        for s in range(1, N_GRP):
            total = total + x_in[s - 1, layer].astype(F32)
        total = total.reshape(N_Z, N_Y, 8, 128)
        for to in range(N_Y):
            y_out[to, layer] = total[:, to].astype(BF)

    loads[0].wait()
    lane = lax.broadcasted_iota(jnp.int32, (64, 128), 1)

    def mark(i, _):
        rows = pl.ds(pl.multiple_of(i * 64, 64), 64)
        wanted = idx[rows, :]
        for k in range(ROWS // 128):
            hot[rows, k * 128:(k + 1) * 128] = jnp.where(wanted == lane + k * 128, 1.0, 0.0).astype(BF)
        return 0

    lax.fori_loop(0, HALO // 64, mark, 0)
    loads[1].wait()
    gather(feat, 0)
    for turn in range(5):
        recv[turn, me] = jnp.zeros((CAP, D), BF)
    pl.semaphore_wait(barrier, N_DOM - 1 + N_GRP - 1)
    exchange(0)
    loads[2].wait()
    gather(hist.at[0], 1)
    exchange(1)
    loads[3].wait()
    gather(hist.at[1], 2)
    exchange(2)

    loads[4].wait()
    for b in range(8):
        tiles = [adj[b, k].astype(F32) for k in range(4)]
        rows = slice(b * 128, (b + 1) * 128)
        for j in range(12):
            if j < 8:
                entry = jnp.where(blk[b, 1] == j, tiles[1], 0.0)
                if j == b:
                    entry = entry + tiles[0]
            else:
                entry = jnp.where(blk[b, 1] == j, tiles[1], 0.0)
                entry = entry + jnp.where(blk[b, 2] == j, tiles[2], 0.0)
                entry = entry + jnp.where(blk[b, 3] == j, tiles[3], 0.0)
            mix[rows, j * 128:(j + 1) * 128] = entry.astype(BF)
            if j < 8:
                back_mix[j * 128:(j + 1) * 128, rows] = entry.T.astype(BF)

    loads[5].wait()
    loads[6].wait()
    back_through(2, cot)

    arrived(0)
    unpack(0)
    forward(0, feat, h1, slope0)
    gather(h1, 3)
    exchange(3)

    arrived(1)
    unpack(1)
    forward(1, h1, h2, slope1)
    gather(h2, 4)
    exchange(4)

    spread(slope1)
    weight_grad(1, grad)
    back_through(1, grad)
    spread(slope0)
    weight_grad(0, grad)
    x_stage(1)
    x_stage(0)

    arrived(2)
    unpack(2)
    forward(2, h2, emb, None)
    emb_copy = pltpu.make_async_copy(emb, emb_o, out_sem.at[0])
    emb_copy.start()
    weight_grad(2, cot)
    y_prepare(1)
    y_prepare(0)
    x_stage(2)
    y_prepare(2)
    for s in range(1, N_Y):
        y_copy(s).start()
    for s in range(1, N_Y):
        y_copy(s).wait_recv()
    total = y_out[y].astype(F32)
    for s in range(1, N_Y):
        total = total + y_in[s - 1].astype(F32)
    for to in range(N_Z):
        z_out[to] = total[:, to].astype(BF)
    for s in range(1, N_Z):
        z_copy(s).start()
    for s in range(1, N_Z):
        z_copy(s).wait_recv()
    total = z_out[z].astype(F32)
    for s in range(1, N_Z):
        total = total + z_in[s - 1].astype(F32)
    quarters[g] = total * (1.0 / math.sqrt(N_GRP * N_DOM * ROWS))
    for s in range(1, N_GRP):
        q_copy(s).start()

    fresh_copies = []
    for turn in (3, 4):
        arrived(turn)
        fresh_copies.append(pltpu.make_async_copy(recv.at[turn], fresh_o.at[turn - 3], out_sem.at[turn - 2]))
        fresh_copies[-1].start()
    for s in range(1, N_GRP):
        q_copy(s).wait_recv()
    for q in range(N_GRP):
        wg_o[:, :, q * 128:(q + 1) * 128] = quarters[q]

    for turn in range(5):
        block = send.at[turn, pl.ds(0, N_DOM - 1)]
        pltpu.make_async_copy(block, block, send_sem.at[turn]).wait()
    for layer in range(3):
        core_copy(layer).wait_send()
        for s in range(1, N_GRP):
            x_copy(layer, s).wait_send()
    for s in range(1, N_Y):
        y_copy(s).wait_send()
    for s in range(1, N_Z):
        z_copy(s).wait_send()
    for s in range(1, N_GRP):
        q_copy(s).wait_send()
    emb_copy.wait()
    for copy in fresh_copies:
        copy.wait()


def body(features, history, adj_tiles, blocks, send_list, counts, weights, cotangent):
    in_use = jnp.arange(CAP, dtype=jnp.int32)[None, :] < counts[0, 0][:, None]
    wanted = jnp.where(in_use, send_list[0, 0], -1).reshape(HALO, 1)
    wanted = jnp.broadcast_to(wanted, (HALO, 128))
    vmem = pltpu.VMEM
    dma = pltpu.SemaphoreType.DMA
    embedding, fresh, grads = pl.pallas_call(
        step_kernel,
        out_shape=(
            jax.ShapeDtypeStruct((ROWS, D), BF),
            jax.ShapeDtypeStruct((2, N_DOM, CAP, D), BF),
            jax.ShapeDtypeStruct((3, 8, D), F32),
        ),
        in_specs=[pl.BlockSpec(memory_space=pltpu.SMEM)] + [pl.BlockSpec(memory_space=pl.ANY)] * 6,
        out_specs=(
            pl.BlockSpec(memory_space=pl.ANY),
            pl.BlockSpec(memory_space=pl.ANY),
            pl.BlockSpec(memory_space=vmem),
        ),
        scratch_shapes=[
            vmem((HALO, 128), jnp.int32),
            vmem((ROWS, D), BF),
            vmem((2, ROWS, D), BF),
            vmem((8, 4, 128, 128), BF),
            vmem((3, D, D), BF),
            vmem((ROWS, D), BF),
            vmem((HALO, ROWS), BF),
            vmem((ROWS, ROWS + HALO), BF),
            vmem((ROWS, ROWS), BF),
            vmem((HALO, D), BF),
            vmem((ROWS, D), BF),
            vmem((ROWS, D), BF),
            vmem((3, ROWS, D), BF),
            vmem((ROWS, D), F32),
            vmem((ROWS, D), F32),
            vmem((ROWS, D), BF),
            vmem((ROWS, D), BF),
            vmem((D, D), F32),
            vmem((ROWS, D), BF),
            vmem((5, N_DOM, CAP, D), BF),
            vmem((5, N_DOM, CAP, D), BF),
            vmem((3, 32, 2, 8, D), BF),
            vmem((3, 32, 8, D), BF),
            vmem((N_GRP, 3, 32, 8, 128), BF),
            vmem((N_GRP - 1, 3, 32, 8, 128), BF),
            vmem((N_Y, 3, N_Z, 8, 128), BF),
            vmem((N_Y - 1, 3, N_Z, 8, 128), BF),
            vmem((N_Z, 3, 8, 128), BF),
            vmem((N_Z - 1, 3, 8, 128), BF),
            vmem((N_GRP, 3, 8, 128), F32),
            dma((7,)),
            dma((5,)),
            dma((5,)),
            dma((2, 3)),
            dma((2, 3, N_GRP - 1)),
            dma((2, N_Y - 1)),
            dma((2, N_Z - 1)),
            dma((2, N_GRP - 1)),
            dma((3,)),
        ],
        compiler_params=pltpu.CompilerParams(
            collective_id=0, has_side_effects=True, vmem_limit_bytes=56 << 20
        ),
        name="graph_step",
    )(blocks[0], wanted, features[0], history[:, 0], adj_tiles[0], weights, cotangent[0])
    return (embedding[None], fresh.reshape(2, 1, HALO, D), grads)


def solution(mesh):
    placed = (
        P("grp", "dom", None),
        P(None, "grp", "dom", None),
        P("grp", "dom", None, None, None),
        P("grp", "dom", None),
        P("grp", "dom", None, None),
        P("grp", "dom", None),
        P(),
        P("grp", "dom", None),
    )
    return jax.shard_map(
        body,
        mesh=mesh,
        in_specs=placed,
        out_specs=(P("grp", "dom", None), P(None, "grp", "dom", None), P(None, "dom", None)),
        check_vma=False,
    )
```

time: 375 us -> 88.1 us (0.23)
  waiting for transfers between devices: 187 us -> 0 us
  Pallas kernels: 0 us -> 78.5 us
  local copies, waits for them, and re-layouts: 57.8 us -> 7.09 us
  starting transfers between devices: 45.3 us -> 0 us
  matrix products: 45.1 us -> 0 us
  other arithmetic: 24.2 us -> 0.74 us
  between operations: 14.3 us -> 0.67 us
    reduce_scatter x1 -> x0, waiting for transfers between devices: 91.7 us -> none  [body(): lax.psum_scatter(replica_total, 'dom', scatter_dimension=1, tiled=True)]
    pallas_call x0 -> x1, Pallas kernels: none -> 78.5 us  [body(): pl.pallas_call(step_kernel, out_shape=(jax.ShapeDtypeStruct((ROWS, D), BF...]
    psum x1 -> x0, waiting for transfers between devices: 53.5 us -> none  [body(): lax.psum(stacked.astype(jnp.bfloat16), 'grp').astype(jnp.float32)]
    dot_general x15 -> x0, matrix products: 45.1 us -> none  [the longest x2 15 us: spread_back(): jnp.dot(owners, contrib_terms.reshape(owners.shape[1], -1), precision=lax...]
    all_to_all x5 -> x0, starting transfers between devices: 45 us -> none  [the longest x1 12.4 us: body(): lax.all_to_all(pack_rows(node_rows, send_rows, live_counts), 'dom', split...]
    all_to_all x5 -> x0, waiting for transfers between devices: 42 us -> none  [the longest x1 14.7 us: body(): lax.all_to_all(pack_rows(hidden_rows[0], send_rows, live_counts), 'dom',...]
    gather x8 -> x0, local copies, waits for them, and re-layouts: 25.7 us -> none  [the longest x5 13.2 us: pack_rows(): picked = jnp.take(source_rows, send_rows.reshape(-1), axis=0)]
    unnamed x32 -> x8, local copies, waits for them, and re-layouts: 23.5 us -> 4.72 us
  transfers between devices with their start and end apart: 7 -> 0, of which waited for: 6 -> 0; matrix products, arithmetic and copies ran while one was open for 15% -> 0% of each run, Pallas kernels for 0% -> 0%
where the time goes in v2:
time: 88.1 us; the launch traced here: 86.9 us
  Pallas kernels  78.5 us (89%)
  local copies, waits for them, and re-layouts  7.09 us (8%)
    pallas_call x1, Pallas kernels, body(): pl.pallas_call(step_kernel, out_shape=(jax.ShapeDtypeStruct((ROWS, D), BF...  78.5 us
    unnamed x8, local copies, waits for them, and re-layouts  4.72 us

profile of v2, /device:TPU:2, one launch (start us, length us, event | category | flops | bytes accessed | tf_op | source)
XLA Modules:
  0.0 86.9 jit_solution(17494702552376472979)
XLA Ops:
  0.6 1.3 %copy.14.blk = s32[8,4]{1,0:T(8,128)} copy(s32[8,4]{0,1:T(4,128)} %bitcast.18) | data formatting | bytes 256 | tf_op jit(solution)/shard_map/squeeze | solution.py:378
  2.0 0.7 iota_compare_fusion
  2.7 0.1 lt.26
  2.8 0.8 copy.13
  3.6 0.1 squeeze.19
  3.7 0.8 broadcast_in_dim.14.idx_h
  4.5 78.5 %graph_step.1 = (bf16[1024,512]{1,0:T(8,128)(2,1)}, bf16[2,64,8,512]{3,2,1,0:T(8,128)(2,1)}, f32[3,8,512]{2,1,0:T(8,128)}) custom-call(s32[8,4]{1,0:T(8,128)} %copy.14.blk, s32[512,128]{1,0:T(8,128)} %broadcast_in_dim.14.idx_h, bf16[1024,512]{1,0:T(8,128)(2,1)} %bitcast.15, bf16[2,1024,512]{2,1,0:T(8,128)(2,1)} %bitcast.12, ...), custom_call_target="tpu_custom_call" | custom-call | tf_op jit(solution)/shard_map/graph_step/pallas_call | solution.py:320
  83.0 0.0 copy-start
  83.0 0.0 copy-start.1
  83.0 2.3 %copy.19 = bf16[1,1024,512]{2,1,0:T(8,128)(2,1)} copy(bf16[1,1024,512]{2,1,0:T(8,128)(2,1)} %bitcast.14) | data formatting | bytes 2097152
  85.4 0.0 copy-done
  85.4 1.0 %copy.20 = bf16[2,1,512,512]{3,2,1,0:T(8,128)(2,1)} copy(bf16[2,1,512,512]{3,2,1,0:T(8,128)(2,1)S(1)} %bitcast.13) | data formatting | bytes 2097152
  86.3 0.0 copy-done.1
  86.3 0.6 copy.21
  (1 shorter events, 0.0 us)
Async XLA Ops:
  83.0 2.4 %copy-start = (bf16[2,64,8,512]{3,2,1,0:T(8,128)(2,1)S(1)}, bf16[2,64,8,512]{3,2,1,0:T(8,128)(2,1)}, u32[]{:S(2)}) copy-start(bf16[2,64,8,512]{3,2,1,0:T(8,128)(2,1)} %get-tuple-element.7) | copy-start | bytes 3145732
  83.0 3.3 %copy-start.1 = (f32[3,8,512]{2,1,0:T(8,128)S(1)}, f32[3,8,512]{2,1,0:T(8,128)}, u32[]{:S(2)}) copy-start(f32[3,8,512]{2,1,0:T(8,128)} %get-tuple-element.20) | copy-start | bytes 147460

commit v3 on v2

v3 whole, which is shorter than its diff:
```python
import functools
import math

import jax
import jax.numpy as jnp
from jax import lax
from jax.experimental import pallas as pl
from jax.experimental.pallas import tpu as pltpu
from jax.sharding import PartitionSpec as P

MESH = pl.DeviceIdType.MESH
BF = jnp.bfloat16
F32 = jnp.float32
N_DOM, N_GRP, N_Z, N_Y = 64, 4, 8, 4
ROWS, D, HALO, CAP = 1024, 512, 512, 8
STEP = 256


def dot(a, b):
    return jnp.dot(a, b, preferred_element_type=F32)


def dot_rows(a, b):
    return lax.dot_general(a, b, (((0,), (0,)), ((), ())), preferred_element_type=F32)


def dot_t(a, b):
    return lax.dot_general(a, b, (((1,), (1,)), ((), ())), preferred_element_type=F32)


def step_kernel(
    blk, list_h, used_h, feat_h, hist_h, adj_h, w_h, cot_h,
    emb, fresh, wg_o,
    rows_of, used, feat, hist, adj, w, cot, hot, mix, back_mix, halo, h1, h2, mid, part, slope0, back2,
    dm, grad, acc, send, recv,
    wg, core_in, x_out, x_in, y_out, y_in, z_out, z_in, quarters,
    in_sem, send_sem, recv_sem, core_sem, x_sem, y_sem, z_sem, q_sem,
):
    me = lax.axis_index("dom")
    g = lax.axis_index("grp")
    z, y, c = me // 8, (me % 8) // 2, me % 2
    loads = [
        pltpu.make_async_copy(a, b, in_sem.at[i])
        for i, (a, b) in enumerate(
            [(list_h, rows_of), (used_h, used), (feat_h, feat), (hist_h.at[0], hist.at[0]), (hist_h.at[1], hist.at[1]),
             (adj_h, adj), (w_h, w), (cot_h, cot)]
        )
    ]
    for load in loads[:3]:
        load.start()

    barrier = pltpu.get_barrier_semaphore()

    def greet(s, _):
        pl.semaphore_signal(barrier, inc=1, device_id={"dom": lax.rem(me + s, N_DOM)}, device_id_type=MESH)
        return 0

    lax.fori_loop(1, N_DOM, greet, 0)
    for s in range(1, N_GRP):
        pl.semaphore_signal(barrier, inc=1, device_id={"grp": lax.rem(g + s, N_GRP)}, device_id_type=MESH)

    for load in loads[3:]:
        load.start()

    def slots(turn):
        return fresh.at[turn - 3] if turn >= 3 else recv.at[turn]

    def gather(rows_ref, turn):
        def one(i, _):
            rows = pl.ds(pl.multiple_of(i * STEP, STEP), STEP)
            picked = dot(hot[rows, :], rows_ref[...])
            send[turn, pl.ds(i * (STEP // CAP), STEP // CAP)] = picked.reshape(STEP // CAP, CAP, D).astype(BF)
            return 0

        lax.fori_loop(0, HALO // STEP, one, 0)

    def exchange(turn):
        def one(s, _):
            half = (s + 1) // 2
            to = jnp.where(lax.rem(s, 2) == 1, lax.rem(me + half, N_DOM), lax.rem(me + N_DOM - half, N_DOM))
            pltpu.make_async_remote_copy(
                send.at[turn, to], slots(turn).at[me], send_sem.at[turn], recv_sem.at[turn],
                device_id={"dom": to}, device_id_type=MESH,
            ).start()
            return 0

        lax.fori_loop(1, N_DOM, one, 0)

    def arrived(turn):
        block = slots(turn).at[pl.ds(0, N_DOM - 1)]
        pltpu.make_async_copy(block, block, recv_sem.at[turn]).wait()

    def unpack(turn):
        def one(i, _):
            part = recv[turn, pl.ds(i * 8, 8)].astype(F32).reshape(64, D)
            halo[pl.ds(pl.multiple_of(i * 64, 64), 64), :] = part.astype(BF)
            return 0

        lax.fori_loop(0, N_DOM // 8, one, 0)

    def own_part(rows_ref):
        def one(i, _):
            rows = pl.ds(pl.multiple_of(i * STEP, STEP), STEP)
            part[rows, :] = dot(mix[rows, 0:ROWS], rows_ref[...])
            return 0

        lax.fori_loop(0, ROWS // STEP, one, 0)

    def forward(layer, next_ref):
        def one(i, _):
            rows = pl.ds(pl.multiple_of(i * STEP, STEP), STEP)
            mixed = (part[rows, :] + dot(mix[rows, ROWS:ROWS + HALO], halo[...])).astype(BF)
            mid[layer, rows, :] = mixed
            value = dot(mixed, w[layer])
            if layer == 2:
                next_ref[rows, :] = value.astype(BF)
            else:
                gate = jax.nn.sigmoid(value)
                next_ref[rows, :] = (value * gate).astype(BF)
                slope = gate * (1.0 + value * (1.0 - gate))
                if layer == 0:
                    slope0[rows, :] = slope
                else:
                    grad[rows, :] = (back2[rows, :] * slope).astype(BF)
            return 0

        lax.fori_loop(0, ROWS // STEP, one, 0)

    def back_through(layer, grad_ref):
        def one(i, _):
            rows = pl.ds(pl.multiple_of(i * STEP, STEP), STEP)
            dm[rows, :] = dot_t(grad_ref[rows, :], w[layer]).astype(BF)
            return 0

        lax.fori_loop(0, ROWS // STEP, one, 0)

    def spread(last):
        def one(i, _):
            rows = pl.ds(pl.multiple_of(i * STEP, STEP), STEP)
            value = dot(back_mix[rows, :], dm[...])
            if last:
                grad[rows, :] = (value * slope0[rows, :]).astype(BF)
            else:
                back2[rows, :] = value
            return 0

        lax.fori_loop(0, ROWS // STEP, one, 0)

    def weight_grad(layer, grad_ref):
        acc[...] = jnp.zeros_like(acc)

        def one(i, _):
            rows = pl.ds(pl.multiple_of(i * STEP, STEP), STEP)
            acc[...] += dot_rows(mid[layer, rows, :], grad_ref[rows, :])
            return 0

        lax.fori_loop(0, ROWS // STEP, one, 0)
        wg[layer] = acc[...].reshape(32, 2, 8, D).astype(BF)
        core_copy(layer).start()

    def core_copy(layer):
        return pltpu.make_async_remote_copy(
            wg.at[layer, :, 1 - c], core_in.at[layer], core_sem.at[0, layer], core_sem.at[1, layer],
            device_id={"dom": me + 1 - 2 * c}, device_id_type=MESH,
        )

    def x_copy(layer, s):
        to = lax.rem(g + s, N_GRP)
        return pltpu.make_async_remote_copy(
            x_out.at[to, layer], x_in.at[s - 1, layer], x_sem.at[0, layer, s - 1], x_sem.at[1, layer, s - 1],
            device_id={"grp": to}, device_id_type=MESH,
        )

    def x_stage(layer):
        core_copy(layer).wait_recv()
        both = wg[layer, :, c].astype(F32) + core_in[layer].astype(F32)
        for q in range(N_GRP):
            x_out[q, layer] = both[:, :, q * 128:(q + 1) * 128].astype(BF)
        for s in range(1, N_GRP):
            x_copy(layer, s).start()

    def y_copy(layer, s):
        to = lax.rem(y + s, N_Y)
        return pltpu.make_async_remote_copy(
            y_out.at[to, layer], y_in.at[s - 1, layer], y_sem.at[0, layer, s - 1], y_sem.at[1, layer, s - 1],
            device_id={"dom": z * 8 + to * 2 + c}, device_id_type=MESH,
        )

    def z_copy(s):
        to = lax.rem(z + s, N_Z)
        return pltpu.make_async_remote_copy(
            z_out.at[to], z_in.at[s - 1], z_sem.at[0, s - 1], z_sem.at[1, s - 1],
            device_id={"dom": to * 8 + y * 2 + c}, device_id_type=MESH,
        )

    def q_copy(s):
        return pltpu.make_async_remote_copy(
            quarters.at[g], quarters.at[g], q_sem.at[0, s - 1], q_sem.at[1, s - 1],
            device_id={"grp": lax.rem(g + s, N_GRP)}, device_id_type=MESH,
        )

    def y_stage(layer):
        for s in range(1, N_GRP):
            x_copy(layer, s).wait_recv()
        total = x_out[g, layer].astype(F32)
        for s in range(1, N_GRP):
            total = total + x_in[s - 1, layer].astype(F32)
        total = total.reshape(N_Z, N_Y, 8, 128)
        for to in range(N_Y):
            y_out[to, layer] = total[:, to].astype(BF)
        for s in range(1, N_Y):
            y_copy(layer, s).start()

    def z_prepare(layer):
        for s in range(1, N_Y):
            y_copy(layer, s).wait_recv()
        total = y_out[y, layer].astype(F32)
        for s in range(1, N_Y):
            total = total + y_in[s - 1, layer].astype(F32)
        for to in range(N_Z):
            z_out[to, layer] = total[to].astype(BF)

    loads[0].wait()
    loads[1].wait()
    slot = lax.broadcasted_iota(jnp.int32, (CAP, N_DOM), 0)
    wanted = jnp.where(slot < used[...], rows_of[...], -1)
    lane = lax.broadcasted_iota(jnp.int32, (2 * CAP, 128), 1)
    for p in range(0, N_DOM, 2):
        pair = jnp.concatenate(
            [jnp.broadcast_to(wanted[:, q:q + 1], (CAP, 128)) for q in (p, p + 1)], axis=0
        )
        for k in range(ROWS // 128):
            hot[p * CAP:(p + 2) * CAP, k * 128:(k + 1) * 128] = jnp.where(pair == lane + k * 128, 1.0, 0.0).astype(BF)
    loads[2].wait()
    gather(feat, 0)
    for turn in range(5):
        slots(turn)[me] = jnp.zeros((CAP, D), BF)
    pl.semaphore_wait(barrier, N_DOM - 1 + N_GRP - 1)
    exchange(0)
    loads[3].wait()
    gather(hist.at[0], 1)
    exchange(1)
    loads[4].wait()
    gather(hist.at[1], 2)
    exchange(2)

    loads[5].wait()
    for b in range(8):
        tiles = [adj[b, k].astype(F32) for k in range(4)]
        rows = slice(b * 128, (b + 1) * 128)
        for j in range(12):
            if j < 8:
                entry = jnp.where(blk[1, b] == j, tiles[1], 0.0)
                if j == b:
                    entry = entry + tiles[0]
            else:
                entry = jnp.where(blk[1, b] == j, tiles[1], 0.0)
                entry = entry + jnp.where(blk[2, b] == j, tiles[2], 0.0)
                entry = entry + jnp.where(blk[3, b] == j, tiles[3], 0.0)
            mix[rows, j * 128:(j + 1) * 128] = entry.astype(BF)
            if j < 8:
                back_mix[j * 128:(j + 1) * 128, rows] = entry.T.astype(BF)

    loads[6].wait()
    loads[7].wait()
    own_part(feat)
    back_through(2, cot)
    spread(False)

    arrived(0)
    unpack(0)
    forward(0, h1)
    gather(h1, 3)
    exchange(3)
    own_part(h1)

    arrived(1)
    unpack(1)
    forward(1, h2)
    gather(h2, 4)
    exchange(4)

    weight_grad(1, grad)
    back_through(1, grad)
    spread(True)
    x_stage(1)
    weight_grad(0, grad)
    own_part(h2)
    x_stage(0)

    arrived(2)
    unpack(2)
    forward(2, emb)
    weight_grad(2, cot)
    y_stage(1)
    x_stage(2)
    y_stage(0)
    z_prepare(1)
    y_stage(2)
    z_prepare(0)
    z_prepare(2)
    for s in range(1, N_Z):
        z_copy(s).start()
    for s in range(1, N_Z):
        z_copy(s).wait_recv()
    total = z_out[z].astype(F32)
    for s in range(1, N_Z):
        total = total + z_in[s - 1].astype(F32)
    quarters[g] = total * (1.0 / math.sqrt(N_GRP * N_DOM * ROWS))
    for s in range(1, N_GRP):
        q_copy(s).start()

    for s in range(1, N_GRP):
        q_copy(s).wait_recv()
    for q in range(N_GRP):
        wg_o[:, :, q * 128:(q + 1) * 128] = quarters[q]

    arrived(3)
    arrived(4)
    for turn in range(5):
        block = send.at[turn, pl.ds(0, N_DOM - 1)]
        pltpu.make_async_copy(block, block, send_sem.at[turn]).wait()
    for layer in range(3):
        core_copy(layer).wait_send()
        for s in range(1, N_GRP):
            x_copy(layer, s).wait_send()
        for s in range(1, N_Y):
            y_copy(layer, s).wait_send()
    for s in range(1, N_Z):
        z_copy(s).wait_send()
    for s in range(1, N_GRP):
        q_copy(s).wait_send()


def out_kernel(emb, fresh, grads, emb_o, fresh_o, grads_o, sem):
    copies = [
        pltpu.make_async_copy(a, b, sem.at[i])
        for i, (a, b) in enumerate([(emb, emb_o), (fresh, fresh_o), (grads, grads_o)])
    ]
    for copy in copies:
        copy.start()
    for copy in copies:
        copy.wait()


def body(features, history, adj_tiles, blocks, send_list, counts, weights, cotangent):
    vmem = pltpu.VMEM
    dma = pltpu.SemaphoreType.DMA
    whole = pl.BlockSpec(memory_space=vmem)
    anywhere = pl.BlockSpec(memory_space=pl.ANY)
    shapes = (((ROWS, D), BF), ((2, N_DOM, CAP, D), BF), ((3, 8, D), F32))
    made = pl.pallas_call(
        step_kernel,
        out_shape=tuple(vmem(*shape) for shape in shapes),
        in_specs=[pl.BlockSpec(memory_space=pltpu.SMEM)] + [anywhere] * 7,
        out_specs=(whole,) * 3,
        scratch_shapes=[
            vmem((CAP, N_DOM), jnp.int32),
            vmem((1, N_DOM), jnp.int32),
            vmem((ROWS, D), BF),
            vmem((2, ROWS, D), BF),
            vmem((8, 4, 128, 128), BF),
            vmem((3, D, D), BF),
            vmem((ROWS, D), BF),
            vmem((HALO, ROWS), BF),
            vmem((ROWS, ROWS + HALO), BF),
            vmem((ROWS, ROWS), BF),
            vmem((HALO, D), BF),
            vmem((ROWS, D), BF),
            vmem((ROWS, D), BF),
            vmem((3, ROWS, D), BF),
            vmem((ROWS, D), F32),
            vmem((ROWS, D), F32),
            vmem((ROWS, D), F32),
            vmem((ROWS, D), BF),
            vmem((ROWS, D), BF),
            vmem((D, D), F32),
            vmem((5, N_DOM, CAP, D), BF),
            vmem((3, N_DOM, CAP, D), BF),
            vmem((3, 32, 2, 8, D), BF),
            vmem((3, 32, 8, D), BF),
            vmem((N_GRP, 3, 32, 8, 128), BF),
            vmem((N_GRP - 1, 3, 32, 8, 128), BF),
            vmem((N_Y, 3, N_Z, 8, 128), BF),
            vmem((N_Y - 1, 3, N_Z, 8, 128), BF),
            vmem((N_Z, 3, 8, 128), BF),
            vmem((N_Z - 1, 3, 8, 128), BF),
            vmem((N_GRP, 3, 8, 128), F32),
            dma((8,)),
            dma((5,)),
            dma((5,)),
            dma((2, 3)),
            dma((2, 3, N_GRP - 1)),
            dma((2, 3, N_Y - 1)),
            dma((2, N_Z - 1)),
            dma((2, N_GRP - 1)),
        ],
        compiler_params=pltpu.CompilerParams(
            collective_id=0, has_side_effects=True, vmem_limit_bytes=56 << 20
        ),
        name="graph_step",
    )(
        blocks[0].T, send_list[0, 0].T, counts[0], features[0], history[:, 0], adj_tiles[0], weights, cotangent[0]
    )
    made = [pltpu.with_memory_space_constraint(piece, pltpu.VMEM) for piece in made]
    embedding, fresh, grads = pl.pallas_call(
        out_kernel,
        out_shape=tuple(jax.ShapeDtypeStruct(*shape) for shape in shapes),
        in_specs=[whole] * 3,
        out_specs=(anywhere,) * 3,
        scratch_shapes=[dma((3,))],
        name="outputs",
    )(*made)
    return (embedding[None], fresh.reshape(2, 1, HALO, D), grads)


def solution(mesh):
    placed = (
        P("grp", "dom", None),
        P(None, "grp", "dom", None),
        P("grp", "dom", None, None, None),
        P("grp", "dom", None),
        P("grp", "dom", None, None),
        P("grp", "dom", None),
        P(),
        P("grp", "dom", None),
    )
    return jax.shard_map(
        body,
        mesh=mesh,
        in_specs=placed,
        out_specs=(P("grp", "dom", None), P(None, "grp", "dom", None), P(None, "dom", None)),
        check_vma=False,
    )
```

time: 88.1 us -> 77.8 us (0.88)
  local copies, waits for them, and re-layouts: 7.09 us -> 0 us
  Pallas kernels: 78.5 us -> 76.3 us
    unnamed x8 -> x0, local copies, waits for them, and re-layouts: 4.72 us -> none
    pallas_call x1 -> x2, Pallas kernels: 78.5 us -> 76.3 us  [the longest x1 75 us: body(): pl.pallas_call(step_kernel, out_shape=tuple((vmem(*shape) for shape in sh...]
    squeeze x2 -> x0, local copies, waits for them, and re-layouts: 1.44 us -> none  [the longest x1 1.35 us: body(): blocks[0]]
where the time goes in v3:
time: 77.8 us; the launch traced here: 76.9 us
  Pallas kernels  76.3 us (98%)
    pallas_call x1, Pallas kernels, body(): pl.pallas_call(step_kernel, out_shape=tuple((vmem(*shape) for shape in sh...  75 us

profile of v3, /device:TPU:2, one launch (start us, length us, event | category | flops | bytes accessed | tf_op | source)
XLA Modules:
  0.0 76.9 jit_solution(13645618672478919)
XLA Ops:
  0.6 75.0 %graph_step.1 = (bf16[1024,512]{1,0:T(8,128)(2,1)S(1)}, bf16[2,64,8,512]{3,2,1,0:T(8,128)(2,1)S(1)}, f32[3,8,512]{2,1,0:T(8,128)S(1)}) custom-call(s32[4,8]{1,0:T(4,128)} %bitcast.20, s32[8,64]{1,0:T(8,128)} %bitcast.19, s32[1,64]{1,0:T(1,128)} %bitcast.21, bf16[1024,512]{1,0:T(8,128)(2,1)} %bitcast.16, bf16[2,1024,512]{2,1,0:T(8,128)(2,1)} %bitcast.15, ...), custom_call_target="tpu_custom_call" | custom-call | tf_op jit(solution)/shard_map/graph_step/pallas_call | solution.py:352
  75.6 1.3 %outputs.1 = (bf16[1024,512]{1,0:T(8,128)(2,1)}, bf16[2,64,8,512]{3,2,1,0:T(8,128)(2,1)}, f32[3,8,512]{2,1,0:T(8,128)}) custom-call(bf16[1024,512]{1,0:T(8,128)(2,1)S(1)} %get-tuple-element.9.emb, bf16[2,64,8,512]{3,2,1,0:T(8,128)(2,1)S(1)} %get-tuple-element.10.fresh, f32[3,8,512]{2,1,0:T(8,128)S(1)} %get-tuple-element.11.grads), custom_call_target="tpu_custom_call" | custom-call | tf_op jit(solution)/shard_map/outputs/pallas_call | solution.py:406

commit v4 on v3

--- a/solution.py
+++ b/solution.py
@@ -13,7 +13,8 @@
 F32 = jnp.float32
 N_DOM, N_GRP, N_Z, N_Y = 64, 4, 8, 4
 ROWS, D, HALO, CAP = 1024, 512, 512, 8
-STEP = 256
+STEP = 1024
+HELD = 32
 
 
 def dot(a, b):
@@ -67,15 +68,16 @@
 
     def gather(rows_ref, turn):
         def one(i, _):
-            rows = pl.ds(pl.multiple_of(i * STEP, STEP), STEP)
+            rows = pl.ds(pl.multiple_of(i * HALO, HALO), HALO)
             picked = dot(hot[rows, :], rows_ref[...])
-            send[turn, pl.ds(i * (STEP // CAP), STEP // CAP)] = picked.reshape(STEP // CAP, CAP, D).astype(BF)
-            return 0
-
-        lax.fori_loop(0, HALO // STEP, one, 0)
-
-    def exchange(turn):
-        def one(s, _):
+            send[turn, pl.ds(i * (HALO // CAP), HALO // CAP)] = picked.reshape(HALO // CAP, CAP, D).astype(BF)
+            return 0
+
+        lax.fori_loop(0, 1, one, 0)
+
+    def exchange(turn, first=1, last=N_DOM):
+        def one(i, _):
+            s = N_DOM - i if turn == 4 else i
             half = (s + 1) // 2
             to = jnp.where(lax.rem(s, 2) == 1, lax.rem(me + half, N_DOM), lax.rem(me + N_DOM - half, N_DOM))
             pltpu.make_async_remote_copy(
@@ -84,7 +86,7 @@
             ).start()
             return 0
 
-        lax.fori_loop(1, N_DOM, one, 0)
+        lax.fori_loop(first, last, one, 0)
 
     def arrived(turn):
         block = slots(turn).at[pl.ds(0, N_DOM - 1)]
@@ -278,7 +280,7 @@
     unpack(1)
     forward(1, h2)
     gather(h2, 4)
-    exchange(4)
+    exchange(4, 1, HELD)
 
     weight_grad(1, grad)
     back_through(1, grad)
@@ -301,6 +303,7 @@
     z_prepare(2)
     for s in range(1, N_Z):
         z_copy(s).start()
+    exchange(4, HELD, N_DOM)
     for s in range(1, N_Z):
         z_copy(s).wait_recv()
     total = z_out[z].astype(F32)

time: 77.8 us -> 75.9 us (0.976); the launches traced: 76.9 us -> 75.8 us
  Pallas kernels: 76.3 us -> 75.2 us
    pallas_call x1, Pallas kernels: 75 us -> 73.9 us  [body(): pl.pallas_call(step_kernel, out_shape=tuple((vmem(*shape) for shape in sh...]
where the time goes in v4:
time: 75.9 us; the launch traced here: 75.8 us
  Pallas kernels  75.2 us (99%)
    pallas_call x1, Pallas kernels, body(): pl.pallas_call(step_kernel, out_shape=tuple((vmem(*shape) for shape in sh...  73.9 us

profile of v4, /device:TPU:2, one launch (start us, length us, event | category | flops | bytes accessed | tf_op | source)
XLA Modules:
  0.0 75.8 jit_solution(15366062604577599037)
XLA Ops:
  0.6 73.9 %graph_step.1 = (bf16[1024,512]{1,0:T(8,128)(2,1)S(1)}, bf16[2,64,8,512]{3,2,1,0:T(8,128)(2,1)S(1)}, f32[3,8,512]{2,1,0:T(8,128)S(1)}) custom-call(s32[4,8]{1,0:T(4,128)} %bitcast.20, s32[8,64]{1,0:T(8,128)} %bitcast.19, s32[1,64]{1,0:T(1,128)} %bitcast.21, bf16[1024,512]{1,0:T(8,128)(2,1)} %bitcast.16, bf16[2,1024,512]{2,1,0:T(8,128)(2,1)} %bitcast.15, ...), custom_call_target="tpu_custom_call" | custom-call | tf_op jit(solution)/shard_map/graph_step/pallas_call | solution.py:355
  74.5 1.3 %outputs.1 = (bf16[1024,512]{1,0:T(8,128)(2,1)}, bf16[2,64,8,512]{3,2,1,0:T(8,128)(2,1)}, f32[3,8,512]{2,1,0:T(8,128)}) custom-call(bf16[1024,512]{1,0:T(8,128)(2,1)S(1)} %get-tuple-element.9.emb, bf16[2,64,8,512]{3,2,1,0:T(8,128)(2,1)S(1)} %get-tuple-element.10.fresh, f32[3,8,512]{2,1,0:T(8,128)S(1)} %get-tuple-element.11.grads), custom_call_target="tpu_custom_call" | custom-call | tf_op jit(solution)/shard_map/outputs/pallas_call | solution.py:409

commit v5 on v4

--- a/solution.py
+++ b/solution.py
@@ -33,7 +33,7 @@
     blk, list_h, used_h, feat_h, hist_h, adj_h, w_h, cot_h,
     emb, fresh, wg_o,
     rows_of, used, feat, hist, adj, w, cot, hot, mix, back_mix, halo, h1, h2, mid, part, slope0, back2,
-    dm, grad, acc, send, recv,
+    dm, grad, send, recv,
     wg, core_in, x_out, x_in, y_out, y_in, z_out, z_in, quarters,
     in_sem, send_sem, recv_sem, core_sem, x_sem, y_sem, z_sem, q_sem,
 ):
@@ -77,7 +77,7 @@
 
     def exchange(turn, first=1, last=N_DOM):
         def one(i, _):
-            s = N_DOM - i if turn == 4 else i
+            s = N_DOM - i
             half = (s + 1) // 2
             to = jnp.where(lax.rem(s, 2) == 1, lax.rem(me + half, N_DOM), lax.rem(me + N_DOM - half, N_DOM))
             pltpu.make_async_remote_copy(
@@ -149,15 +149,7 @@
         lax.fori_loop(0, ROWS // STEP, one, 0)
 
     def weight_grad(layer, grad_ref):
-        acc[...] = jnp.zeros_like(acc)
-
-        def one(i, _):
-            rows = pl.ds(pl.multiple_of(i * STEP, STEP), STEP)
-            acc[...] += dot_rows(mid[layer, rows, :], grad_ref[rows, :])
-            return 0
-
-        lax.fori_loop(0, ROWS // STEP, one, 0)
-        wg[layer] = acc[...].reshape(32, 2, 8, D).astype(BF)
+        wg[layer] = dot_rows(mid[layer], grad_ref[...]).reshape(32, 2, 8, D).astype(BF)
         core_copy(layer).start()
 
     def core_copy(layer):
@@ -377,7 +369,6 @@
             vmem((ROWS, D), F32),
             vmem((ROWS, D), BF),
             vmem((ROWS, D), BF),
-            vmem((D, D), F32),
             vmem((5, N_DOM, CAP, D), BF),
             vmem((3, N_DOM, CAP, D), BF),
             vmem((3, 32, 2, 8, D), BF),

time: 75.9 us -> 76 us (level)
  no operation moved by 1% of the time
where the time goes in v5:
time: 76 us; the launch traced here: 75.9 us
  Pallas kernels  75.3 us (99%)
    pallas_call x1, Pallas kernels, body(): pl.pallas_call(step_kernel, out_shape=tuple((vmem(*shape) for shape in sh...  73.9 us

profile of v5, /device:TPU:2, one launch (start us, length us, event | category | flops | bytes accessed | tf_op | source)
XLA Modules:
  0.0 75.9 jit_solution(9012206028661764502)
XLA Ops:
  0.6 73.9 %graph_step.1 = (bf16[1024,512]{1,0:T(8,128)(2,1)S(1)}, bf16[2,64,8,512]{3,2,1,0:T(8,128)(2,1)S(1)}, f32[3,8,512]{2,1,0:T(8,128)S(1)}) custom-call(s32[4,8]{1,0:T(4,128)} %bitcast.20, s32[8,64]{1,0:T(8,128)} %bitcast.19, s32[1,64]{1,0:T(1,128)} %bitcast.21, bf16[1024,512]{1,0:T(8,128)(2,1)} %bitcast.16, bf16[2,1024,512]{2,1,0:T(8,128)(2,1)} %bitcast.15, ...), custom_call_target="tpu_custom_call" | custom-call | tf_op jit(solution)/shard_map/graph_step/pallas_call | solution.py:347
  74.6 1.3 %outputs.1 = (bf16[1024,512]{1,0:T(8,128)(2,1)}, bf16[2,64,8,512]{3,2,1,0:T(8,128)(2,1)}, f32[3,8,512]{2,1,0:T(8,128)}) custom-call(bf16[1024,512]{1,0:T(8,128)(2,1)S(1)} %get-tuple-element.9.emb, bf16[2,64,8,512]{3,2,1,0:T(8,128)(2,1)S(1)} %get-tuple-element.10.fresh, f32[3,8,512]{2,1,0:T(8,128)S(1)} %get-tuple-element.11.grads), custom_call_target="tpu_custom_call" | custom-call | tf_op jit(solution)/shard_map/outputs/pallas_call | solution.py:400
